TPU v7x, 32 devices: a whole 2x2x4 slice. The times are simulated.
32 devices in a mesh: req: 4 (over z), exp: 8 (over y, x, core).
Axes of the slice: x: 2, y: 2, z: 4, core: 2. Of those that a mesh axis runs over, the one named last changes fastest.
Arguments:
- queries: bfloat16 [64, 32, 2304], P(('req', 'exp')), may hold values from -8 to 8
- draft_keys: bfloat16 [64, 32, 2304], P(('req', 'exp')), may hold values from -9 to 9
- draft_values: bfloat16 [64, 32, 2304], P(('req', 'exp')), may hold values from -6 to 6
- tree_parents: int32 [64, 32], P(('req', 'exp')), may hold values from -1 to 30, as said below
- cache_keys: bfloat16 [64, 768, 2304], P(('req', 'exp')), may hold values from -9 to 9
- cache_values: bfloat16 [64, 768, 2304], P(('req', 'exp')), may hold values from -6 to 6
- cache_lengths: int32 [64], P(('req', 'exp')), may hold values from 1 to 768, as said below
- prompt_keys: bfloat16 [8, 512, 2304], P('req', 'exp'), may hold values from -9 to 9
- prompt_values: bfloat16 [8, 512, 2304], P('req', 'exp'), may hold values from -6 to 6
- group_ids: int32 [64], P(('req', 'exp')), may hold values from 0 to 1
- residual: bfloat16 [64, 32, 2304], P(('req', 'exp')), may hold values from -6 to 6
- norm_gain: float32 [2304], replicated, may hold values from 0.5 to 1.5
- router: bfloat16 [2304, 8], replicated, may hold values from -0.125 to 0.125
- w_gate: bfloat16 [8, 2304, 5760], P('exp', None, 'req'), may hold values from -0.125 to 0.125
- w_up: bfloat16 [8, 2304, 5760], P('exp', None, 'req'), may hold values from -0.125 to 0.125
- w_down: bfloat16 [8, 5760, 2304], P('exp', 'req'), may hold values from -0.078125 to 0.078125
- expert_ids: int32 [64, 32, 2], P(('req', 'exp')), may hold values from 0 to 7, all different within a row; in each aligned block of 64 rows (0 to 63, 64 to 127, ..., all dimensions but the last counted through in order) at most 18 rows name the same one
- accepted_rows: int32 [64, 8], P(('req', 'exp')), may hold values from 0 to 31
Outputs:
- attended: bfloat16 [64, 32, 2304], P(('req', 'exp'))
- layer_out: bfloat16 [64, 32, 2304], P(('req', 'exp'))
- accepted_cache: bfloat16 [64, 2, 8, 2304], P(('req', 'exp'))
Inputs may be any that keep to these rules, and one draw needn't show every extreme that they name: `tree_parents`: position 0 of every tree holds -1; every other position holds an earlier position of the same tree. `cache_lengths`: some request has all 768 slots used. `expert_ids`: the two experts of a position differ; among the rows of one device no expert is named more than 18 times, a bound that some block reaches.
All inputs are finite; a program needn't handle non-finite values.
Results may differ from a plain program's by a relative error of at most 0.013.
Values may be sent and summed in bfloat16 or wider, within the bound.
A program may use at most 192 MiB of HBM per device.

v0:
```python
import jax
import jax.numpy as jnp
from jax import lax
from jax.sharding import PartitionSpec as P

HEADS = 36
HDIM = 64
EXPERTS = 8
TOPK = 2
GRP = 2
CAP = 18
HIGH = lax.Precision.HIGHEST
EPSILON = 1e-05


def ancestry(parents):
    length = parents.shape[-1]
    column = jnp.arange(length, dtype=jnp.int32)
    reached = (parents[..., :, None] == column).astype(jnp.float32) + jnp.eye(
        length, dtype=jnp.float32
    )
    for repeat in range(max(1, (length - 1).bit_length())):
        reached = (jnp.einsum("...ij,...jk->...ik", reached, reached, precision=HIGH) > 0.5).astype(
            jnp.float32
        )
    return reached > 0.5


def slot_numbers(picked_ids):
    flattened = picked_ids.reshape(-1)
    onehot = (flattened[:, None] == jnp.arange(EXPERTS, dtype=jnp.int32)[None, :]).astype(jnp.int32)
    before = jnp.cumsum(onehot, axis=0) - onehot
    return jnp.sum(before * onehot, axis=1).reshape(picked_ids.shape)


def on_device(
    queries,
    draft_keys,
    draft_values,
    tree_parents,
    cache_keys,
    cache_values,
    cache_lengths,
    prompt_keys,
    prompt_values,
    group_ids,
    residual,
    norm_gain,
    router,
    w_gate,
    w_up,
    w_down,
    expert_ids,
    accepted_rows,
):
    requests, tree_len, width = queries.shape
    row_count = requests * tree_len
    score_scale = HDIM ** (-0.5)
    heads_q = queries.reshape(requests, tree_len, HEADS, HDIM)
    cache_heads = cache_keys.reshape(requests, -1, HEADS, HDIM)
    cache_vals = cache_values.reshape(requests, -1, HEADS, HDIM)
    cache_scores = (
        jnp.einsum("bthd,bchd->bthc", heads_q, cache_heads, preferred_element_type=jnp.float32)
        * score_scale
    )
    live_cache = jnp.arange(cache_heads.shape[1], dtype=jnp.int32)[None, :] < cache_lengths[:, None]
    cache_scores = jnp.where(live_cache[:, None, None, :], cache_scores, -jnp.inf)
    draft_heads = draft_keys.reshape(requests, tree_len, HEADS, HDIM)
    draft_vals = draft_values.reshape(requests, tree_len, HEADS, HDIM)
    tree_scores = (
        jnp.einsum("bthd,bshd->bths", heads_q, draft_heads, preferred_element_type=jnp.float32)
        * score_scale
    )
    tree_scores = jnp.where(ancestry(tree_parents)[:, :, None, :], tree_scores, -jnp.inf)
    local_top = jnp.maximum(jnp.max(cache_scores, axis=-1), jnp.max(tree_scores, axis=-1))
    cache_weights = jnp.exp(cache_scores - local_top[..., None])
    tree_weights = jnp.exp(tree_scores - local_top[..., None])
    local_total = jnp.sum(cache_weights, axis=-1) + jnp.sum(tree_weights, axis=-1)
    local_acc = jnp.einsum(
        "bthc,bchd->bthd",
        cache_weights.astype(jnp.bfloat16),
        cache_vals,
        preferred_element_type=jnp.float32,
    )
    local_acc = local_acc + jnp.einsum(
        "bths,bshd->bthd",
        tree_weights.astype(jnp.bfloat16),
        draft_vals,
        preferred_element_type=jnp.float32,
    )
    local_top = local_top.reshape(row_count, HEADS)
    local_total = local_total.reshape(row_count, HEADS)
    local_acc = local_acc.reshape(row_count, HEADS, HDIM)
    member = jnp.repeat(group_ids, tree_len)[:, None] == jnp.arange(GRP, dtype=jnp.int32)[None, :]
    query_rows = heads_q.reshape(row_count, HEADS, HDIM)
    running_top = local_top
    summed = local_total
    gathered_acc = local_acc
    key_piece = lax.all_gather(prompt_keys, "exp", axis=1, tiled=True)
    value_piece = lax.all_gather(prompt_values, "exp", axis=1, tiled=True)
    key_count = key_piece.shape[1]
    key_heads = key_piece.reshape(GRP, key_count, HEADS, HDIM)
    value_heads = value_piece.reshape(GRP, key_count, HEADS, HDIM)
    block_scores = (
        jnp.einsum("rhd,gkhd->rhgk", query_rows, key_heads, preferred_element_type=jnp.float32)
        * score_scale
    )
    block_scores = jnp.where(member[:, None, :, None], block_scores, -jnp.inf)
    new_top = jnp.maximum(running_top, jnp.max(block_scores, axis=(2, 3)))
    shrink = jnp.exp(running_top - new_top)
    block_weights = jnp.exp(block_scores - new_top[:, :, None, None])
    summed = summed * shrink + jnp.sum(block_weights, axis=(2, 3))
    gathered_acc = gathered_acc * shrink[:, :, None] + jnp.einsum(
        "rhgk,gkhd->rhd",
        block_weights.astype(jnp.bfloat16),
        value_heads,
        preferred_element_type=jnp.float32,
    )
    running_top, summed, gathered_acc = (new_top, summed, gathered_acc)
    attended = (
        (gathered_acc / summed[:, :, None]).reshape(requests, tree_len, width).astype(jnp.bfloat16)
    )
    stream = (residual.astype(jnp.float32) + attended.astype(jnp.float32)).astype(jnp.bfloat16)
    stream_rows = stream.reshape(row_count, width).astype(jnp.float32)
    normed = (
        stream_rows
        * lax.rsqrt(jnp.mean(stream_rows * stream_rows, axis=-1, keepdims=True) + EPSILON)
        * norm_gain
    ).astype(jnp.bfloat16)
    logits = jnp.dot(normed, router, preferred_element_type=jnp.float32)
    routed = expert_ids.reshape(row_count, TOPK)
    chosen = jnp.take_along_axis(logits, routed, axis=1)
    gate_first = 1.0 / (1.0 + jnp.exp(chosen[:, 1] - chosen[:, 0]))
    gates = jnp.stack([gate_first, 1.0 - gate_first], axis=1)
    target = routed * CAP + slot_numbers(routed)
    buffer = (
        jnp.zeros((EXPERTS * CAP, width), jnp.bfloat16)
        .at[target.reshape(-1)]
        .set(jnp.repeat(normed, TOPK, axis=0))
    )
    holder_count = lax.axis_size("exp")
    holders = holder_count // EXPERTS
    outgoing = jnp.broadcast_to(
        buffer.reshape(EXPERTS, 1, CAP, width), (EXPERTS, holders, CAP, width)
    ).reshape(holder_count, CAP, width)
    gate_local = w_gate[0]
    up_local = w_up[0]
    down_local = w_down[0]
    arrived = lax.all_to_all(outgoing, "exp", split_axis=0, concat_axis=0, tiled=True)
    row_piece = lax.all_gather(arrived.reshape(-1, width), "req", axis=0, tiled=True)
    gate_proj = jnp.dot(row_piece, gate_local, preferred_element_type=jnp.float32)
    up_proj = jnp.dot(row_piece, up_local, preferred_element_type=jnp.float32)
    hidden = (jax.nn.silu(gate_proj) * up_proj).astype(jnp.bfloat16)
    summed_rows = lax.psum_scatter(
        jnp.dot(hidden, down_local, preferred_element_type=jnp.float32).astype(jnp.bfloat16),
        "req",
        scatter_dimension=0,
        tiled=True,
    )
    returned = lax.all_to_all(
        summed_rows.reshape(holder_count, CAP, width),
        "exp",
        split_axis=0,
        concat_axis=0,
        tiled=True,
    )
    expert_result = (
        returned.astype(jnp.float32)
        .reshape(EXPERTS, holders, CAP, width)
        .sum(axis=1)
        .reshape(EXPERTS * CAP, width)
    )
    picked = expert_result[target]
    layer_out = (
        (stream_rows + jnp.sum(gates[:, :, None] * picked, axis=1))
        .astype(jnp.bfloat16)
        .reshape(requests, tree_len, width)
    )
    kept_keys = jnp.take_along_axis(draft_keys, accepted_rows[:, :, None], axis=1)
    kept_values = jnp.take_along_axis(draft_values, accepted_rows[:, :, None], axis=1)
    accepted_cache = jnp.stack([kept_keys, kept_values], axis=1)
    return (attended, layer_out, accepted_cache)


def solution(mesh):
    return jax.shard_map(
        on_device,
        mesh=mesh,
        in_specs=(
            P(("req", "exp"), None, None),
            P(("req", "exp"), None, None),
            P(("req", "exp"), None, None),
            P(("req", "exp"), None),
            P(("req", "exp"), None, None),
            P(("req", "exp"), None, None),
            P(("req", "exp")),
            P("req", "exp", None),
            P("req", "exp", None),
            P(("req", "exp")),
            P(("req", "exp"), None, None),
            P(),
            P(),
            P("exp", None, "req"),
            P("exp", None, "req"),
            P("exp", "req", None),
            P(("req", "exp"), None, None),
            P(("req", "exp"), None),
        ),
        out_specs=(
            P(("req", "exp"), None, None),
            P(("req", "exp"), None, None),
            P(("req", "exp"), None, None, None),
        ),
        check_vma=False,
    )
```

profile of v0, /device:TPU:0, one launch (start us, length us, event | category | flops | bytes accessed | tf_op | source)
XLA Modules:
  0.0 296.1 jit_solution(12981081108997633056)
XLA Ops:
  7.2 2.5 copy.75
  9.8 2.5 copy.79
  12.4 1.4 reshape.291
  13.8 2.5 reshape_reshape.6
  16.4 10.3 %copy.70 = bf16[2,768,2304]{1,2,0:T(8,128)(2,1)} copy(bf16[2,768,2304]{2,1,0:T(8,128)(2,1)} %param.25) | data formatting | bytes 14155776 | tf_op args[5]
  26.7 10.4 %copy.65 = bf16[2,768,2304]{1,2,0:T(8,128)(2,1)} copy(bf16[2,768,2304]{2,1,0:T(8,128)(2,1)} %param.24) | data formatting | bytes 14155776 | tf_op args[4]
  38.6 1.4 reshape.294
  40.0 1.4 fusion.107
  41.4 4.9 %bitcast_reduce_fusion = (f32[2,32,36]{1,2,0:T(8,128)S(1)}, f32[2,36,768,32]{2,3,1,0:T(8,128)S(1)}) fusion(pred[2,768]{1,0:T(4,128)(4,1)S(1)} %iota_compare_fusion.4, bf16[2,768,36,64]{1,3,2,0:T(8,128)(2,1)} %bitcast.124, bf16[2,32,36,64]{3,2,1,0:T(8,128)(2,1)} %copy-done.10), kind=kOutput, calls=%fused_computation.11 | convolution fusion | flops 231798528 | bytes 14461440 | tf_op jit(solution)/shard_map/bthd,bchd->bthc/dot_general | solution.py:63
  46.4 3.3 %fusion.24 = f32[2,36,32,64]{3,2,1,0:T(8,128)} fusion(bf16[2,768,36,64]{1,3,2,0:T(8,128)(2,1)S(1)} %bitcast.128, f32[2,36,768,32]{2,3,1,0:T(8,128)S(1)} %get-tuple-element.15, f32[2,32,36]{1,2,0:T(8,128)S(1)} %max.36, pred[2,768]{1,0:T(4,128)(4,1)S(1)} %iota_compare_fusion.4), kind=kOutput, calls=%fused_computation.31 | convolution fusion | flops 233570304 | bytes 14756352 | tf_op jit(solution)/shard_map/bthc,bchd->bthd/dot_general | solution.py:79
  49.7 2.4 fusion.37
  52.9 4.0 %fusion.10 = f32[2,32,36]{1,2,0:T(8,128)S(1)} fusion(f32[2,36,768,32]{2,3,1,0:T(8,128)} %copy-done.2, f32[2,32,36]{1,2,0:T(8,128)S(1)} %max.36, pred[2,768]{1,0:T(4,128)(4,1)S(1)} %iota_compare_fusion.4), kind=kLoop, calls=%fused_computation.20 | loop fusion | flops 7075584 | bytes 7097856 | tf_op jit(solution)/shard_map/reduce_sum | solution.py:78
  58.0 12.5 %copy.76 = bf16[2,512,2304]{1,2,0:T(8,128)(2,1)} copy(bf16[2,512,2304]{2,0,1:T(2,128)(2,1)} %all-gather.4.cloned.1.call-done) | data formatting | bytes 9437184 | tf_op jit(solution)/shard_map/all_gather | solution.py:99
  70.5 3.4 %fusion.2 = (f32[64,36]{0,1:T(8,128)S(1)}, f32[36,2,512,64]{2,3,1,0:T(8,128)S(1)}) fusion(pred[64,2]{0,1:T(4,128)(4,1)S(1)} %iota_compare_fusion.5, bf16[2,512,36,64]{1,3,2,0:T(8,128)(2,1)} %bitcast.125, bf16[64,36,64,1]{2,1,0,3:T(8,128)(2,1)S(1)} %bitcast.130), kind=kOutput, calls=%fused_computation.9 | convolution fusion | flops 309065472 | bytes 14460032 | tf_op jit(solution)/shard_map/rhd,gkhd->rhgk/dot_general | solution.py:105
  73.9 2.3 fusion
  76.2 1.6 copy-done.1
  78.1 14.3 %all-gather.6.cloned.1.call-done = bf16[2,512,2304]{2,0,1:T(2,128)(2,1)} async-done(((bf16[2,64,2304]{2,0,1:T(2,128)(2,1)}), bf16[2,512,2304]{2,0,1:T(2,128)(2,1)}) %all-gather.6.cloned.1.call-update) | async-done | bytes 4718608 | tf_op jit(solution)/shard_map/all_gather | solution.py:100
  92.4 12.4 %copy.80 = bf16[2,512,2304]{1,2,0:T(8,128)(2,1)} copy(bf16[2,512,2304]{2,0,1:T(2,128)(2,1)} %all-gather.6.cloned.1.call-done) | data formatting | bytes 9437184 | tf_op jit(solution)/shard_map/all_gather | solution.py:100
  104.8 7.3 %divide_convert_fusion = bf16[64,36,64]{2,0,1:T(8,128)(2,1)S(1)} fusion(f32[64,36,64]{2,0,1:T(8,128)S(1)} %bitcast_multiply_fusion, bf16[2,512,36,64]{1,3,2,0:T(8,128)(2,1)} %bitcast.129, f32[36,2,512,64]{2,3,1,0:T(8,128)} %copy-done.1, f32[64,36]{0,1:T(8,128)S(1)} %max.38, pred[64,2]{0,1:T(4,128)(4,1)S(1)} %iota_compare_fusion.5, ...), kind=kOutput, calls=%fused_computation.46 | convolution fusion | flops 311869440 | bytes 15059072 | tf_op jit(solution)/shard_map/rhgk,gkhd->rhd/dot_general | solution.py:113
  113.9 1.6 scatter_custom_fusion
  115.7 16.2 %all_to_all.10 = bf16[8,18,2304]{2,1,0:T(8,128)(2,1)S(1)} all-to-all(bf16[8,18,2304]{2,1,0:T(8,128)(2,1)S(1)} %reshape_reshape.7), channel_id=1, replica_groups=mesh['req'=4,'exp'=8] {'exp'}, dimensions={0} | all-to-all | bytes 1327104 | tf_op jit(solution)/shard_map/all_to_all | solution.py:149
  131.9 1.0 reshape.301
  133.0 54.6 %all-gather.8.cloned.1.call-done = bf16[576,2304]{1,0:T(8,128)(2,1)} async-done(((bf16[144,2304]{1,0:T(8,128)(2,1)}), bf16[576,2304]{1,0:T(8,128)(2,1)}) %all-gather.8.cloned.1.call-update) | async-done | bytes 2654224 | tf_op jit(solution)/shard_map/all_gather | solution.py:150
  187.6 9.7 %fusion.8 = f32[576,1440]{1,0:T(8,128)} fusion(bf16[576,2304]{1,0:T(8,128)(2,1)} %all-gather.8.cloned.1.call-done, bf16[1,2304,1440]{1,2,0:T(8,128)(2,1)} %param.33), kind=kOutput, calls=%fused_computation.18 | convolution fusion | flops 3822059520 | bytes 12607488 | tf_op jit(solution)/shard_map/dot_general | solution.py:151
  197.3 16.7 %fusion.21 = bf16[576,2304]{1,0:T(8,128)(2,1)} fusion(bf16[1,1440,2304]{2,1,0:T(8,128)(2,1)} %param.35, f32[576,1440]{1,0:T(8,128)} %fusion.8, bf16[576,2304]{1,0:T(8,128)(2,1)} %all-gather.8.cloned.1.call-done, bf16[1,2304,1440]{1,2,0:T(8,128)(2,1)} %param.34), kind=kOutput, calls=%fused_computation.30 | convolution fusion | flops 7650422784 | bytes 21897216 | tf_op jit(solution)/shard_map/dot_general | solution.py:155
  217.4 48.2 %reduce-scatter.2.cloned.1.call-done = bf16[144,2304]{1,0:T(8,128)(2,1)} async-done(((bf16[576,2304]{1,0:T(8,128)(2,1)}), bf16[144,2304]{1,0:T(8,128)(2,1)}) %reduce-scatter.2.cloned.1.call-update) | async-done | bytes 663568 | tf_op jit(solution)/shard_map/reduce_scatter | solution.py:154
  265.6 2.2 reshape.302
  267.8 3.8 %all-to-all-start.1 = ((bf16[8,18,2304]{2,1,0:T(8,128)(2,1)}), bf16[8,18,2304]{2,1,0:T(8,128)(2,1)S(1)}, u32[]{:S(2)}, u32[]{:S(2)}) async-start(bf16[8,18,2304]{2,1,0:T(8,128)(2,1)} %reshape.302), calls=%async_computation.2 | async-start | bytes 1769472 | tf_op jit(solution)/shard_map/all_to_all | solution.py:160
  271.7 1.1 gather_fusion.1
  273.2 11.9 %all-to-all-done.1 = bf16[8,18,2304]{2,1,0:T(8,128)(2,1)S(1)} async-done(((bf16[8,18,2304]{2,1,0:T(8,128)(2,1)}), bf16[8,18,2304]{2,1,0:T(8,128)(2,1)S(1)}, u32[]{:S(2)}, u32[]{:S(2)}) %all-to-all-start.1) | async-done | bytes 663584 | tf_op jit(solution)/shard_map/all_to_all | solution.py:160
  285.3 1.1 gather_fusion
  287.1 1.6 multiply_reduce_fusion
  (124 shorter events, 11.4 us)
Async XLA Ops:
  7.2 264.4 %copy-start = (bf16[2304,8]{0,1:T(8,128)(2,1)S(1)}, bf16[2304,8]{0,1:T(8,128)(2,1)}, u32[]{:S(2)}) copy-start(bf16[2304,8]{0,1:T(8,128)(2,1)} %param.32) | copy-start | bytes 110596
  7.2 50.8 %all-gather.4.cloned.1.call-start = ((), (), s32[]{:S(2)}) async-start(), calls=%async_computation.3 | async-start | bytes 5308416 | tf_op jit(solution)/shard_map/all_gather | solution.py:99
  9.8 82.6 %all-gather.6.cloned.1.call-start = ((), (), s32[]{:S(2)}) async-start(), calls=%async_computation.4 | async-start | bytes 5308416 | tf_op jit(solution)/shard_map/all_gather | solution.py:100
  12.3 175.2 %all-gather.8.cloned.1.call-start = ((), (), s32[]{:S(2)}) async-start(), calls=%async_computation.5 | async-start | bytes 3317760 | tf_op jit(solution)/shard_map/all_gather | solution.py:150
  13.8 26.2 %copy-start.10 = (bf16[2,32,36,64]{3,2,1,0:T(8,128)(2,1)}, bf16[2,32,36,64]{3,2,1,0:T(8,128)(2,1)S(1)}, u32[]{:S(2)}) copy-start(bf16[2,32,36,64]{3,2,1,0:T(8,128)(2,1)S(1)} %reshape.291) | copy-start | bytes 884740
  26.7 10.4 %copy-start.4 = (bf16[2,32,2304]{2,1,0:T(8,128)(2,1)S(1)}, bf16[2,32,2304]{2,1,0:T(8,128)(2,1)}, u32[]{:S(2)}) copy-start(bf16[2,32,2304]{2,1,0:T(8,128)(2,1)} %param.21) | copy-start | bytes 884740
  26.7 10.9 %copy-start.17 = (s32[2,32]{1,0:T(2,128)S(1)}, s32[2,32]{1,0:T(2,128)}, u32[]{:S(2)}) copy-start(s32[2,32]{1,0:T(2,128)} %param.23) | copy-start | bytes 772
  26.7 11.9 %copy-start.5 = (bf16[2,32,2304]{2,1,0:T(8,128)(2,1)S(1)}, bf16[2,32,2304]{2,1,0:T(8,128)(2,1)}, u32[]{:S(2)}) copy-start(bf16[2,32,2304]{2,1,0:T(8,128)(2,1)} %param.22) | copy-start | bytes 884740
  26.7 13.2 %copy-start.16 = (s32[2]{0:T(128)S(1)}, s32[2]{0:T(128)}, u32[]{:S(2)}) copy-start(s32[2]{0:T(128)} %param.26) | copy-start | bytes 28
  40.0 6.4 %slice-start = ((s8[7077888]{0:T(1024)(128)(4,1)}), s8[4194304]{0:T(1024)(128)(4,1)S(1)}, s32[]{:S(2)}) async-start(s8[7077888]{0:T(1024)(128)(4,1)} %bitcast.126), calls=%async_computation.7 | async-start | bytes 8388608
  41.4 5.0 %slice-start.1 = ((s8[7077888]{0:T(1024)(128)(4,1)}), s8[2883584]{0:T(1024)(128)(4,1)S(1)}, s32[]{:S(2)}) async-start(s8[7077888]{0:T(1024)(128)(4,1)} %bitcast.126), calls=%async_computation.8 | async-start | bytes 5767168
  46.3 3.4 %copy-start.2 = (f32[2,36,768,32]{2,3,1,0:T(8,128)}, f32[2,36,768,32]{2,3,1,0:T(8,128)S(1)}, u32[]{:S(2)}) copy-start(f32[2,36,768,32]{2,3,1,0:T(8,128)S(1)} %get-tuple-element.15) | copy-start | bytes 21233668
  49.7 2.6 copy-start.18
  49.7 2.8 copy-start.3
  52.3 4.7 %copy-start.13 = (s32[2,32,2]{1,2,0:T(2,128)S(1)}, s32[2,32,2]{1,2,0:T(2,128)}, u32[]{:S(2)}) copy-start(s32[2,32,2]{1,2,0:T(2,128)} %param.36) | copy-start | bytes 1540
  57.9 12.5 %copy-start.9 = (bf16[64,36,64]{2,1,0:T(8,128)(2,1)S(1)}, bf16[64,36,64]{2,1,0:T(8,128)(2,1)}, u32[]{:S(2)}) copy-start(bf16[64,36,64]{2,1,0:T(8,128)(2,1)} %reshape_reshape.6) | copy-start | bytes 884740
  73.8 3.9 %copy-start.1 = (f32[36,2,512,64]{2,3,1,0:T(8,128)}, f32[36,2,512,64]{2,3,1,0:T(8,128)S(1)}, u32[]{:S(2)}) copy-start(f32[36,2,512,64]{2,3,1,0:T(8,128)S(1)} %get-tuple-element.19) | copy-start | bytes 28311556
  104.8 8.1 %copy-start.11 = (bf16[2,32,2304]{2,1,0:T(8,128)(2,1)S(1)}, bf16[2,32,2304]{2,1,0:T(8,128)(2,1)}, u32[]{:S(2)}) copy-start(bf16[2,32,2304]{2,1,0:T(8,128)(2,1)} %param.30) | copy-start | bytes 884740
  104.8 8.5 %copy-start.14 = (f32[2304]{0:T(1024)S(1)}, f32[2304]{0:T(1024)}, u32[]{:S(2)}) copy-start(f32[2304]{0:T(1024)} %param.31) | copy-start | bytes 27652
  112.9 1.0 copy-start.7
  133.0 132.6 %reduce-scatter.2.cloned.1.call-start = ((), (), s32[]{:S(2)}) async-start(), calls=%async_computation.6 | async-start | bytes 3317760 | tf_op jit(solution)/shard_map/reduce_scatter | solution.py:154
  197.3 17.0 %copy-start.15 = (s32[2,8]{1,0:T(2,128)S(1)}, s32[2,8]{1,0:T(2,128)}, u32[]{:S(2)}) copy-start(s32[2,8]{1,0:T(2,128)} %param.37) | copy-start | bytes 196
  197.3 17.9 %copy-start.6 = (bf16[2,32,2304]{2,1,0:T(8,128)(2,1)S(1)}, bf16[2,32,2304]{2,1,0:T(8,128)(2,1)}, u32[]{:S(2)}) copy-start(bf16[2,32,2304]{2,1,0:T(8,128)(2,1)} %param.22) | copy-start | bytes 884740
  267.8 17.3 %all-to-all-start.1 = ((bf16[8,18,2304]{2,1,0:T(8,128)(2,1)}), bf16[8,18,2304]{2,1,0:T(8,128)(2,1)S(1)}, u32[]{:S(2)}, u32[]{:S(2)}) async-start(bf16[8,18,2304]{2,1,0:T(8,128)(2,1)} %reshape.302), calls=%async_computation.2 | async-start | bytes 1769472 | tf_op jit(solution)/shard_map/all_to_all | solution.py:160
  285.3 3.5 %copy-start.8 = (bf16[2,32,2304]{2,1,0:T(8,128)(2,1)S(1)}, bf16[2,32,2304]{2,1,0:T(8,128)(2,1)}, u32[]{:S(2)}) copy-start(bf16[2,32,2304]{2,1,0:T(8,128)(2,1)} %copy-done.7) | copy-start | bytes 884740
  285.3 3.5 %copy-start.12 = (bf16[2,32,2304]{2,1,0:T(8,128)(2,1)S(1)}, bf16[2,32,2304]{2,1,0:T(8,128)(2,1)}, u32[]{:S(2)}) copy-start(bf16[2,32,2304]{2,1,0:T(8,128)(2,1)} %param.30) | copy-start | bytes 884740
Sparse Core Ops, SparseCore 0:
  9.9 41.6 all-gather.3
  53.4 38.9 all-gather.5
  133.1 54.4 all-gather.7
  214.2 51.3 reduce-scatter.1
where the time goes:
time: 298 us; the launch traced here: 296 us
  waiting for transfers between devices  129 us (43%)
  local copies, waits for them, and re-layouts  71.3 us (24%)
  matrix products  50.2 us (17%)
  blocking collectives  16.2 us (5%)
  between operations  14.3 us (5%)
  other arithmetic  11.3 us (4%)
  starting transfers between devices  3.93 us (1%)
    all_gather x1, waiting for transfers between devices, on_device(): lax.all_gather(arrived.reshape(-1, width), 'req', axis=0, tiled=True)  54.6 us
    reduce_scatter x1, waiting for transfers between devices, on_device(): lax.psum_scatter(jnp.dot(hidden, down_local, preferred_element_type=jnp.f...  48.2 us
    unnamed x48, local copies, waits for them, and re-layouts  27.5 us
    dot_general x1, matrix products, on_device(): jnp.dot(hidden, down_local, preferred_element_type=jnp.float32)  16.7 us
    all_to_all x1, blocking collectives, on_device(): lax.all_to_all(outgoing, 'exp', split_axis=0, concat_axis=0, tiled=True)  16.2 us
    all_gather x1, waiting for transfers between devices, on_device(): value_piece = lax.all_gather(prompt_values, 'exp', axis=1, tiled=True)  14.3 us
    all_gather x1, local copies, waits for them, and re-layouts, on_device(): key_piece = lax.all_gather(prompt_keys, 'exp', axis=1, tiled=True)  12.5 us
    all_gather x1, local copies, waits for them, and re-layouts, on_device(): value_piece = lax.all_gather(prompt_values, 'exp', axis=1, tiled=True)  12.4 us
  transfers between devices with their start and end apart: 5, of which 4 were waited for; matrix products, arithmetic and copies ran while one was open for 24% of the time, Pallas kernels for 0%

commit v1 on v0

--- a/solution.py
+++ b/solution.py
@@ -11,6 +11,22 @@
 CAP = 18
 HIGH = lax.Precision.HIGHEST
 EPSILON = 1e-05
+
+
+def ring_gather(x, axis, dim):
+    ways, here, step = (lax.axis_size(axis), lax.axis_index(axis), x.shape[dim])
+    dims = [n * ways if d == dim else n for d, n in enumerate(x.shape)]
+    full = lax.dynamic_update_slice_in_dim(jnp.zeros(dims, x.dtype), x, here * step, axis=dim)
+    going_up = going_down = x
+    for far in range(1, ways // 2 + 1):
+        going_up = lax.ppermute(going_up, axis, [(d, (d + 1) % ways) for d in range(ways)])
+        full = lax.dynamic_update_slice_in_dim(full, going_up, (here - far) % ways * step, axis=dim)
+        if 2 * far < ways:
+            going_down = lax.ppermute(going_down, axis, [(d, (d - 1) % ways) for d in range(ways)])
+            full = lax.dynamic_update_slice_in_dim(
+                full, going_down, (here + far) % ways * step, axis=dim
+            )
+    return full
 
 
 def ancestry(parents):
@@ -147,7 +163,7 @@
     up_local = w_up[0]
     down_local = w_down[0]
     arrived = lax.all_to_all(outgoing, "exp", split_axis=0, concat_axis=0, tiled=True)
-    row_piece = lax.all_gather(arrived.reshape(-1, width), "req", axis=0, tiled=True)
+    row_piece = ring_gather(arrived.reshape(-1, width), "req", 0)
     gate_proj = jnp.dot(row_piece, gate_local, preferred_element_type=jnp.float32)
     up_proj = jnp.dot(row_piece, up_local, preferred_element_type=jnp.float32)
     hidden = (jax.nn.silu(gate_proj) * up_proj).astype(jnp.bfloat16)

time: 298 us -> 288 us (0.966)
  waiting for transfers between devices: 129 us -> 118 us
  starting transfers between devices: 3.93 us -> 7.81 us
    all_gather x1 -> x0, waiting for transfers between devices: 54.6 us -> none  [on_device(): lax.all_gather(arrived.reshape(-1, width), 'req', axis=0, tiled=True)]
    ppermute x0 -> x3, waiting for transfers between devices: none -> 42.6 us  [the longest x2 29.7 us: ring_gather(): lax.ppermute(going_up, axis, [(d, (d + 1) % ways) for d in range(ways)])]
    ppermute x0 -> x3, starting transfers between devices: none -> 3.88 us  [the longest x1 2.34 us: ring_gather(): lax.ppermute(going_down, axis, [(d, (d - 1) % ways) for d in range(ways)])]
    unnamed x48 -> x52, local copies, waits for them, and re-layouts: 27.5 us -> 28.6 us
  transfers between devices with their start and end apart: 5 -> 7, of which waited for: 4 -> 6; matrix products, arithmetic and copies ran while one was open for 24% -> 24% of each run, Pallas kernels for 0% -> 0%
where the time goes in v1:
time: 288 us; the launch traced here: 287 us
  waiting for transfers between devices  118 us (41%)
  local copies, waits for them, and re-layouts  69.9 us (24%)
  matrix products  49.3 us (17%)
  blocking collectives  16.1 us (6%)
  between operations  14.4 us (5%)
  other arithmetic  11.2 us (4%)
  starting transfers between devices  7.81 us (3%)
    reduce_scatter x1, waiting for transfers between devices, on_device(): lax.psum_scatter(jnp.dot(hidden, down_local, preferred_element_type=jnp.f...  46.9 us
    ppermute x2, waiting for transfers between devices, ring_gather(): lax.ppermute(going_up, axis, [(d, (d + 1) % ways) for d in range(ways)])  29.7 us
    unnamed x52, local copies, waits for them, and re-layouts  28.6 us
    all_gather x1, waiting for transfers between devices, on_device(): value_piece = lax.all_gather(prompt_values, 'exp', axis=1, tiled=True)  16.7 us
    dot_general x1, matrix products, on_device(): jnp.dot(hidden, down_local, preferred_element_type=jnp.float32)  16.7 us
    all_to_all x1, blocking collectives, on_device(): lax.all_to_all(outgoing, 'exp', split_axis=0, concat_axis=0, tiled=True)  16.1 us
    ppermute x1, waiting for transfers between devices, ring_gather(): lax.ppermute(going_down, axis, [(d, (d - 1) % ways) for d in range(ways)])  12.9 us
    all_gather x1, local copies, waits for them, and re-layouts, on_device(): key_piece = lax.all_gather(prompt_keys, 'exp', axis=1, tiled=True)  12.6 us
  transfers between devices with their start and end apart: 7, of which 6 were waited for; matrix products, arithmetic and copies ran while one was open for 24% of the time, Pallas kernels for 0%

profile of v1, /device:TPU:0, one launch (start us, length us, event | category | flops | bytes accessed | tf_op | source)
XLA Modules:
  0.0 286.9 jit_solution(8805141274731233207)
XLA Ops:
  7.2 2.5 copy.75
  9.9 2.5 copy.79
  12.9 1.4 reshape_reshape.6
  14.3 10.2 %copy.70 = bf16[2,768,2304]{1,2,0:T(8,128)(2,1)} copy(bf16[2,768,2304]{2,1,0:T(8,128)(2,1)} %param.25) | data formatting | bytes 14155776 | tf_op args[5]
  24.5 10.3 %copy.65 = bf16[2,768,2304]{1,2,0:T(8,128)(2,1)} copy(bf16[2,768,2304]{2,1,0:T(8,128)(2,1)} %param.24) | data formatting | bytes 14155776 | tf_op args[4]
  36.3 1.4 reshape.294
  37.8 1.5 fusion.108
  39.2 4.9 %bitcast_reduce_fusion = (f32[2,32,36]{1,2,0:T(8,128)S(1)}, f32[2,36,768,32]{2,3,1,0:T(8,128)S(1)}) fusion(pred[2,768]{1,0:T(4,128)(4,1)S(1)} %iota_compare_fusion.4, bf16[2,768,36,64]{1,3,2,0:T(8,128)(2,1)} %bitcast.124, bf16[2,32,36,64]{3,2,1,0:T(8,128)(2,1)} %copy-done.11), kind=kOutput, calls=%fused_computation.11 | convolution fusion | flops 231798528 | bytes 14461440 | tf_op jit(solution)/shard_map/bthd,bchd->bthc/dot_general | solution.py:79
  44.3 3.3 %fusion.24 = f32[2,36,32,64]{3,2,1,0:T(8,128)} fusion(bf16[2,768,36,64]{1,3,2,0:T(8,128)(2,1)S(1)} %bitcast.128, f32[2,36,768,32]{2,3,1,0:T(8,128)S(1)} %get-tuple-element.15, f32[2,32,36]{1,2,0:T(8,128)S(1)} %max.36, pred[2,768]{1,0:T(4,128)(4,1)S(1)} %iota_compare_fusion.4), kind=kOutput, calls=%fused_computation.31 | convolution fusion | flops 233570304 | bytes 14756352 | tf_op jit(solution)/shard_map/bthc,bchd->bthd/dot_general | solution.py:95
  47.6 2.4 fusion.36
  50.7 4.0 %fusion.10 = f32[2,32,36]{1,2,0:T(8,128)S(1)} fusion(f32[2,36,768,32]{2,3,1,0:T(8,128)} %copy-done.2, f32[2,32,36]{1,2,0:T(8,128)S(1)} %max.36, pred[2,768]{1,0:T(4,128)(4,1)S(1)} %iota_compare_fusion.4), kind=kLoop, calls=%fused_computation.20 | loop fusion | flops 7075584 | bytes 7097856 | tf_op jit(solution)/shard_map/reduce_sum | solution.py:94
  55.8 12.6 %copy.76 = bf16[2,512,2304]{1,2,0:T(8,128)(2,1)} copy(bf16[2,512,2304]{2,0,1:T(2,128)(2,1)} %all-gather.3.cloned.1.call-done) | data formatting | bytes 9437184 | tf_op jit(solution)/shard_map/all_gather | solution.py:115
  68.3 3.4 %fusion.2 = (f32[64,36]{0,1:T(8,128)S(1)}, f32[36,2,512,64]{2,3,1,0:T(8,128)S(1)}) fusion(pred[64,2]{0,1:T(4,128)(4,1)S(1)} %iota_compare_fusion.5, bf16[2,512,36,64]{1,3,2,0:T(8,128)(2,1)} %bitcast.125, bf16[64,36,64,1]{2,1,0,3:T(8,128)(2,1)S(1)} %bitcast.130), kind=kOutput, calls=%fused_computation.9 | convolution fusion | flops 309065472 | bytes 14460032 | tf_op jit(solution)/shard_map/rhd,gkhd->rhgk/dot_general | solution.py:121
  71.7 2.3 fusion
  75.7 16.7 %all-gather.5.cloned.1.call-done = bf16[2,512,2304]{2,0,1:T(2,128)(2,1)} async-done(((bf16[2,64,2304]{2,0,1:T(2,128)(2,1)}), bf16[2,512,2304]{2,0,1:T(2,128)(2,1)}) %all-gather.5.cloned.1.call-update) | async-done | bytes 4718608 | tf_op jit(solution)/shard_map/all_gather | solution.py:116
  92.4 12.4 %copy.80 = bf16[2,512,2304]{1,2,0:T(8,128)(2,1)} copy(bf16[2,512,2304]{2,0,1:T(2,128)(2,1)} %all-gather.5.cloned.1.call-done) | data formatting | bytes 9437184 | tf_op jit(solution)/shard_map/all_gather | solution.py:116
  104.8 7.3 %divide_convert_fusion = bf16[64,36,64]{2,0,1:T(8,128)(2,1)S(1)} fusion(f32[64,36,64]{2,0,1:T(8,128)S(1)} %bitcast_multiply_fusion, bf16[2,512,36,64]{1,3,2,0:T(8,128)(2,1)} %bitcast.129, f32[36,2,512,64]{2,3,1,0:T(8,128)} %copy-done.1, f32[64,36]{0,1:T(8,128)S(1)} %max.38, pred[64,2]{0,1:T(4,128)(4,1)S(1)} %iota_compare_fusion.5, ...), kind=kOutput, calls=%fused_computation.47 | convolution fusion | flops 311869440 | bytes 15059072 | tf_op jit(solution)/shard_map/rhgk,gkhd->rhd/dot_general | solution.py:129
  113.9 1.6 scatter_custom_fusion
  115.8 16.1 %all_to_all.10 = bf16[8,18,2304]{2,1,0:T(8,128)(2,1)S(1)} all-to-all(bf16[8,18,2304]{2,1,0:T(8,128)(2,1)S(1)} %reshape_reshape.7), channel_id=1, replica_groups=mesh['req'=4,'exp'=8] {'exp'}, dimensions={0} | all-to-all | bytes 1327104 | tf_op jit(solution)/shard_map/all_to_all | solution.py:165
  132.1 1.5 collective-permute-start
  133.6 2.3 collective-permute-start.1
  136.2 15.6 %collective-permute-done = bf16[144,2304]{1,0:T(8,128)(2,1)S(1)} collective-permute-done((bf16[144,2304]{1,0:T(8,128)(2,1)S(1)}, bf16[144,2304]{1,0:T(8,128)(2,1)S(1)}, u32[]{:S(2)}, u32[]{:S(2)}) %collective-permute-start) | collective-permute-done | bytes 663584 | tf_op jit(solution)/shard_map/ppermute | solution.py:22
  151.9 12.9 %collective-permute-done.1 = bf16[144,2304]{1,0:T(8,128)(2,1)S(1)} collective-permute-done((bf16[144,2304]{1,0:T(8,128)(2,1)S(1)}, bf16[144,2304]{1,0:T(8,128)(2,1)S(1)}, u32[]{:S(2)}, u32[]{:S(2)}) %collective-permute-start.1) | collective-permute-done | bytes 663584 | tf_op jit(solution)/shard_map/ppermute | solution.py:25
  164.8 14.1 %collective-permute-done.2 = bf16[144,2304]{1,0:T(8,128)(2,1)S(1)} collective-permute-done((bf16[144,2304]{1,0:T(8,128)(2,1)S(1)}, bf16[144,2304]{1,0:T(8,128)(2,1)S(1)}, u32[]{:S(2)}, u32[]{:S(2)}) %collective-permute-start.2) | collective-permute-done | bytes 663584 | tf_op jit(solution)/shard_map/ppermute | solution.py:22
  179.0 1.6 copy-done.4
  180.5 8.9 %fusion.6 = f32[576,1440]{1,0:T(8,128)} fusion(bf16[576,2304]{1,0:T(8,128)(2,1)S(1)} %constant_dynamic-update-slice_fusion, bf16[1,2304,1440]{1,2,0:T(8,128)(2,1)} %param.34), kind=kOutput, calls=%fused_computation.16 | convolution fusion | flops 3822059520 | bytes 12607488 | tf_op jit(solution)/shard_map/dot_general | solution.py:168
  189.5 16.7 %fusion.21 = bf16[576,2304]{1,0:T(8,128)(2,1)} fusion(bf16[1,1440,2304]{2,1,0:T(8,128)(2,1)} %param.35, f32[576,1440]{1,0:T(8,128)} %fusion.6, bf16[576,2304]{1,0:T(8,128)(2,1)} %copy-done.4, bf16[1,2304,1440]{1,2,0:T(8,128)(2,1)} %param.33), kind=kOutput, calls=%fused_computation.30 | convolution fusion | flops 7650422784 | bytes 21897216 | tf_op jit(solution)/shard_map/dot_general | solution.py:171
  209.5 46.9 %reduce-scatter.2.cloned.1.call-done = bf16[144,2304]{1,0:T(8,128)(2,1)} async-done(((bf16[576,2304]{1,0:T(8,128)(2,1)}), bf16[144,2304]{1,0:T(8,128)(2,1)}) %reduce-scatter.2.cloned.1.call-update) | async-done | bytes 663568 | tf_op jit(solution)/shard_map/reduce_scatter | solution.py:170
  256.4 2.2 reshape.302
  258.6 3.8 %all-to-all-start.1 = ((bf16[8,18,2304]{2,1,0:T(8,128)(2,1)}), bf16[8,18,2304]{2,1,0:T(8,128)(2,1)S(1)}, u32[]{:S(2)}, u32[]{:S(2)}) async-start(bf16[8,18,2304]{2,1,0:T(8,128)(2,1)} %reshape.302), calls=%async_computation.2 | async-start | bytes 1769472 | tf_op jit(solution)/shard_map/all_to_all | solution.py:176
  264.0 11.9 %all-to-all-done.1 = bf16[8,18,2304]{2,1,0:T(8,128)(2,1)S(1)} async-done(((bf16[8,18,2304]{2,1,0:T(8,128)(2,1)}), bf16[8,18,2304]{2,1,0:T(8,128)(2,1)S(1)}, u32[]{:S(2)}, u32[]{:S(2)}) %all-to-all-start.1) | async-done | bytes 663584 | tf_op jit(solution)/shard_map/all_to_all | solution.py:176
  277.9 1.6 multiply_reduce_fusion
  (136 shorter events, 15.8 us)
Async XLA Ops:
  7.2 255.3 %copy-start = (bf16[2304,8]{0,1:T(8,128)(2,1)S(1)}, bf16[2304,8]{0,1:T(8,128)(2,1)}, u32[]{:S(2)}) copy-start(bf16[2304,8]{0,1:T(8,128)(2,1)} %param.32) | copy-start | bytes 110596
  7.2 5.2 %copy-start.12 = (bf16[2,32,2304]{2,1,0:T(8,128)(2,1)S(1)}, bf16[2,32,2304]{2,1,0:T(8,128)(2,1)}, u32[]{:S(2)}) copy-start(bf16[2,32,2304]{2,1,0:T(8,128)(2,1)} %param.20) | copy-start | bytes 884740
  7.2 48.6 %all-gather.3.cloned.1.call-start = ((), (), s32[]{:S(2)}) async-start(), calls=%async_computation.3 | async-start | bytes 5308416 | tf_op jit(solution)/shard_map/all_gather | solution.py:115
  9.8 82.6 %all-gather.5.cloned.1.call-start = ((), (), s32[]{:S(2)}) async-start(), calls=%async_computation.4 | async-start | bytes 5308416 | tf_op jit(solution)/shard_map/all_gather | solution.py:116
  12.4 244.1 %reduce-scatter.2.cloned.1.call-start = ((), (), s32[]{:S(2)}) async-start(), calls=%async_computation.5 | async-start | bytes 3317760 | tf_op jit(solution)/shard_map/reduce_scatter | solution.py:170
  12.9 24.9 %copy-start.11 = (bf16[2,32,36,64]{3,2,1,0:T(8,128)(2,1)}, bf16[2,32,36,64]{3,2,1,0:T(8,128)(2,1)S(1)}, u32[]{:S(2)}) copy-start(bf16[2,32,36,64]{3,2,1,0:T(8,128)(2,1)S(1)} %reshape.291) | copy-start | bytes 884740
  24.5 10.4 %copy-start.5 = (bf16[2,32,2304]{2,1,0:T(8,128)(2,1)S(1)}, bf16[2,32,2304]{2,1,0:T(8,128)(2,1)}, u32[]{:S(2)}) copy-start(bf16[2,32,2304]{2,1,0:T(8,128)(2,1)} %param.21) | copy-start | bytes 884740
  24.5 10.8 %copy-start.19 = (s32[2,32]{1,0:T(2,128)S(1)}, s32[2,32]{1,0:T(2,128)}, u32[]{:S(2)}) copy-start(s32[2,32]{1,0:T(2,128)} %param.23) | copy-start | bytes 772
  24.5 11.8 %copy-start.6 = (bf16[2,32,2304]{2,1,0:T(8,128)(2,1)S(1)}, bf16[2,32,2304]{2,1,0:T(8,128)(2,1)}, u32[]{:S(2)}) copy-start(bf16[2,32,2304]{2,1,0:T(8,128)(2,1)} %param.22) | copy-start | bytes 884740
  24.5 13.2 %copy-start.18 = (s32[2]{0:T(128)S(1)}, s32[2]{0:T(128)}, u32[]{:S(2)}) copy-start(s32[2]{0:T(128)} %param.26) | copy-start | bytes 28
  37.8 6.5 %slice-start = ((s8[7077888]{0:T(1024)(128)(4,1)}), s8[4194304]{0:T(1024)(128)(4,1)S(1)}, s32[]{:S(2)}) async-start(s8[7077888]{0:T(1024)(128)(4,1)} %bitcast.126), calls=%async_computation.6 | async-start | bytes 8388608
  39.2 5.0 %slice-start.1 = ((s8[7077888]{0:T(1024)(128)(4,1)}), s8[2883584]{0:T(1024)(128)(4,1)S(1)}, s32[]{:S(2)}) async-start(s8[7077888]{0:T(1024)(128)(4,1)} %bitcast.126), calls=%async_computation.7 | async-start | bytes 5767168
  44.2 3.4 %copy-start.2 = (f32[2,36,768,32]{2,3,1,0:T(8,128)}, f32[2,36,768,32]{2,3,1,0:T(8,128)S(1)}, u32[]{:S(2)}) copy-start(f32[2,36,768,32]{2,3,1,0:T(8,128)S(1)} %get-tuple-element.15) | copy-start | bytes 21233668
  47.6 2.5 copy-start.20
  47.6 2.7 copy-start.3
  50.6 4.1 %copy-start.15 = (s32[2,32,2]{1,2,0:T(2,128)S(1)}, s32[2,32,2]{1,2,0:T(2,128)}, u32[]{:S(2)}) copy-start(s32[2,32,2]{1,2,0:T(2,128)} %param.36) | copy-start | bytes 1540
  55.7 12.6 %copy-start.10 = (bf16[64,36,64]{2,1,0:T(8,128)(2,1)S(1)}, bf16[64,36,64]{2,1,0:T(8,128)(2,1)}, u32[]{:S(2)}) copy-start(bf16[64,36,64]{2,1,0:T(8,128)(2,1)} %reshape_reshape.6) | copy-start | bytes 884740
  71.7 3.6 %copy-start.1 = (f32[36,2,512,64]{2,3,1,0:T(8,128)}, f32[36,2,512,64]{2,3,1,0:T(8,128)S(1)}, u32[]{:S(2)}) copy-start(f32[36,2,512,64]{2,3,1,0:T(8,128)S(1)} %get-tuple-element.19) | copy-start | bytes 28311556
  104.8 8.1 %copy-start.13 = (bf16[2,32,2304]{2,1,0:T(8,128)(2,1)S(1)}, bf16[2,32,2304]{2,1,0:T(8,128)(2,1)}, u32[]{:S(2)}) copy-start(bf16[2,32,2304]{2,1,0:T(8,128)(2,1)} %param.30) | copy-start | bytes 884740
  104.8 8.5 %copy-start.16 = (f32[2304]{0:T(1024)S(1)}, f32[2304]{0:T(1024)}, u32[]{:S(2)}) copy-start(f32[2304]{0:T(1024)} %param.31) | copy-start | bytes 27652
  112.9 1.0 copy-start.8
  132.1 19.7 %collective-permute-start = (bf16[144,2304]{1,0:T(8,128)(2,1)S(1)}, bf16[144,2304]{1,0:T(8,128)(2,1)S(1)}, u32[]{:S(2)}, u32[]{:S(2)}) collective-permute-start(bf16[144,2304]{1,0:T(8,128)(2,1)S(1)} %reshape.301), channel_id=1, source_target_pairs={{0,8},{8,16},{16,24},{24,0},{1,9},{9,17},{17,25},{25,1},{2,10},{10... | collective-permute-start | bytes 1990664 | tf_op jit(solution)/shard_map/ppermute | solution.py:22
  133.6 31.1 %collective-permute-start.1 = (bf16[144,2304]{1,0:T(8,128)(2,1)S(1)}, bf16[144,2304]{1,0:T(8,128)(2,1)S(1)}, u32[]{:S(2)}, u32[]{:S(2)}) collective-permute-start(bf16[144,2304]{1,0:T(8,128)(2,1)S(1)} %reshape.301), channel_id=1, source_target_pairs={{0,24},{8,0},{16,8},{24,16},{1,25},{9,1},{17,9},{25,17},{2,26},{10... | collective-permute-start | bytes 1990664 | tf_op jit(solution)/shard_map/ppermute | solution.py:25
  151.8 27.1 %collective-permute-start.2 = (bf16[144,2304]{1,0:T(8,128)(2,1)S(1)}, bf16[144,2304]{1,0:T(8,128)(2,1)S(1)}, u32[]{:S(2)}, u32[]{:S(2)}) collective-permute-start(bf16[144,2304]{1,0:T(8,128)(2,1)S(1)} %collective-permute-done), channel_id=1, source_target_pairs={{0,8},{8,16},{16,24},{24,0},{1,9},{9,17},{17,25},{25,1},{2,10},{10... | collective-permute-start | bytes 1990664 | tf_op jit(solution)/shard_map/ppermute | solution.py:22
  178.9 1.6 copy-start.4
  189.5 17.0 %copy-start.17 = (s32[2,8]{1,0:T(2,128)S(1)}, s32[2,8]{1,0:T(2,128)}, u32[]{:S(2)}) copy-start(s32[2,8]{1,0:T(2,128)} %param.37) | copy-start | bytes 196
  206.1 1.2 copy-start.7
  258.6 17.3 %all-to-all-start.1 = ((bf16[8,18,2304]{2,1,0:T(8,128)(2,1)}), bf16[8,18,2304]{2,1,0:T(8,128)(2,1)S(1)}, u32[]{:S(2)}, u32[]{:S(2)}) async-start(bf16[8,18,2304]{2,1,0:T(8,128)(2,1)} %reshape.302), calls=%async_computation.2 | async-start | bytes 1769472 | tf_op jit(solution)/shard_map/all_to_all | solution.py:176
  277.2 2.4 copy-start.9
  277.2 2.4 copy-start.14
Sparse Core Ops, SparseCore 0:
  9.9 41.6 all-gather.2
  53.5 38.9 all-gather.4
  206.3 50.0 reduce-scatter.1
